TPU v7x, 256 devices: a whole 4x4x8 slice. The times are simulated.
256 devices in a mesh: leaf: 2 (over core), row: 16 (over z, x_lo), col: 8 (over y, x_hi).
Axes of the slice: x: 4 (x_hi: 2, x_lo: 2; x = x_hi * 2 + x_lo), y: 4, z: 8, core: 2. Of those that a mesh axis runs over, the one named last changes fastest.
Arguments:
- child_tiles: float32 [1024, 64, 4096], P(('leaf', 'row'), None, 'col'), may hold values from -0.078125 to 0.078125
- block_mask: int32 [1024, 64], P(('leaf', 'row'), 'col'), may hold values 0 or 1
- destination: int32 [1024, 1], P(('leaf', 'row')), may hold values from 0 to 31; in each aligned block of 32 rows (0 to 31, 32 to 63, ...) at most 2 rows name the same one
Outputs:
- r_top: float32 [2, 128, 4096], P('leaf', None, 'col')
Inputs may be any that keep to these rules, and one draw needn't show every extreme that they name: Among the tiles of one device, no destination is named more than 2 times, a bound that some block reaches.
All inputs are finite; a program needn't handle non-finite values. No bound on the sum of `block_mask` on one device may be relied on, other than what follows from the above.
Results may differ from a plain program's by a relative error of at most 0.0003.
Values sent between devices are 32-bit elements; how exact they have to be, the bound alone decides.
A program may use at most 64 MiB of HBM per device.

v0:
```python
import jax
import jax.numpy as jnp
from jax import lax
from jax.sharding import PartitionSpec as P

FRONTS = 2


def per_device(child_tiles, block_mask, destination):
    tile_count, edge, columns_dev = child_tiles.shape
    blocks_dev = columns_dev // edge
    col = lax.axis_index("col")
    per_front = lax.axis_size("row")
    mask = block_mask.astype(jnp.float32)
    rows = tile_count * edge
    tiles = child_tiles.reshape(rows, columns_dev)
    own = tiles[:, :edge] * jnp.repeat(mask[:, 0], edge)[:, None]
    panel = jnp.concatenate([jnp.where(col == k, own, 0.0) for k in range(2)], axis=1)
    panel = lax.psum(panel, "col")
    front = jnp.repeat(destination[:, 0] // per_front, edge)[:, None]
    left = jnp.concatenate([jnp.where(front == f, panel, 0.0) for f in range(FRONTS)], axis=1)
    masked = (tiles.reshape(tile_count, edge, blocks_dev, edge) * mask[:, None, :, None]).reshape(
        rows, columns_dev
    )
    dot = lambda a, b: lax.dot_general(
        a, b, (((0,), (0,)), ((), ())), precision=lax.Precision.HIGHEST
    )
    sums = jnp.concatenate([dot(left, masked), dot(left, panel)], axis=1)
    sums = lax.psum_scatter(sums, "leaf", scatter_dimension=0, tiled=True)
    sums = lax.psum(sums, "row")
    cross, gram = (sums[:, :columns_dev], sums[:, columns_dev:])
    lower = jnp.linalg.cholesky(gram)
    top = lax.linalg.triangular_solve(lower, cross, left_side=True, lower=True)
    col_count = lax.axis_size("col")
    place = jnp.repeat(jnp.arange(blocks_dev) * col_count + col, edge)
    line = jnp.arange(2 * edge) // edge
    return jnp.where(place[None, :] >= line[:, None], top, 0.0)[None]


def solution(mesh):
    in_specs = (
        P(("leaf", "row"), None, "col"),
        P(("leaf", "row"), "col"),
        P(("leaf", "row"), None),
    )
    return jax.shard_map(
        per_device, mesh=mesh, in_specs=in_specs, out_specs=P("leaf", None, "col"), check_vma=False
    )
```

profile of v0, /device:TPU:6, one launch (start us, length us, event | category | flops | bytes accessed | tf_op | source)
XLA Modules:
  0.0 309.4 jit_solution(1366986369914015669)
XLA Ops:
  6.5 0.0 copy-start.1
  6.5 0.0 all-reduce.3.cloned.1.call-start
  6.5 0.7 convert_element_type.3
  7.2 0.1 broadcast_in_dim.48
  7.3 0.1 mul.25
  7.4 1.6 fusion.5
  9.0 1.3 pad_maximum_fusion.3
  10.3 0.0 all-reduce.3.cloned.1.call-update
  10.3 0.0 reduce-scatter.2.cloned.1.call-start
  10.3 0.1 copy.4
  10.4 0.0 copy-done.1
  10.5 0.1 broadcast_in_dim.51
  10.5 0.1 eq.37
  10.6 0.1 broadcast_in_dim.46
  10.7 0.1 eq.33
  10.8 3.8 %mul.28 = f32[32,64,8,64]{3,2,1,0:T(8,128)} broadcast(f32[32,8]{1,0:T(8,128)S(1)} %copy.4), dimensions={0,2} | broadcast | bytes 4195328 | tf_op jit(solution)/shard_map/mul | solution.py:22
  14.6 7.5 %mul.29 = f32[2048,512]{1,0:T(8,128)} reshape(f32[32,64,8,64]{3,2,1,0:T(8,128)} %mul.28) | data formatting | bytes 8388608 | tf_op jit(solution)/shard_map/mul | solution.py:22
  22.1 84.0 %all-reduce.3.cloned.1.call-done = f32[2048,128]{1,0:T(8,128)} async-done(((f32[2048,128]{1,0:T(8,128)}), f32[2048,128]{1,0:T(8,128)}) %all-reduce.3.cloned.1.call-update) | async-done | bytes 1048592 | tf_op jit(solution)/shard_map/psum | solution.py:19
  106.1 2.8 broadcast_select_fusion.1
  109.0 0.0 copy-start
  109.0 9.4 %fusion = f32[256,512]{0,1:T(8,128)S(1)} fusion(f32[2048,512]{1,0:T(8,128)} %bitcast.27, f32[2048,512]{1,0:T(8,128)} %mul.29, f32[2048,128]{1,0:T(8,128)S(1)} %get-tuple-element.10, f32[2048,128]{1,0:T(8,128)S(1)} %get-tuple-element.9), kind=kOutput, calls=%fused_computation | convolution fusion | flops 3222798336 | bytes 11010048 | tf_op jit(solution)/shard_map/dot_general | solution.py:25
  118.4 0.0 copy-done
  118.4 1.9 fusion.2
  120.3 0.9 pad_maximum_fusion.4
  121.2 0.0 reduce-scatter.2.cloned.1.call-update
  121.2 0.2 all-reduce.5.cloned.1.call-start
  121.4 14.5 %reduce-scatter.2.cloned.1.call-done = f32[128,640]{0,1:T(8,128)} async-done(((f32[256,640]{0,1:T(8,128)}), f32[128,640]{0,1:T(8,128)}) %reduce-scatter.2.cloned.1.call-update) | async-done | bytes 327696 | tf_op jit(solution)/shard_map/reduce_scatter | solution.py:29
  136.0 0.0 all-reduce.5.cloned.1.call-update
  136.0 0.1 broadcast_in_dim.45
  136.1 0.1 ge.17
  136.2 140.0 %all-reduce.5.cloned.1.call-done = f32[128,640]{0,1:T(8,128)} async-done(((f32[128,640]{0,1:T(8,128)}), f32[128,640]{0,1:T(8,128)}) %all-reduce.5.cloned.1.call-update) | async-done | bytes 327696 | tf_op jit(solution)/shard_map/psum | solution.py:30
  276.1 0.8 slice.25
  277.0 0.1 copy.6
  277.1 0.9 fusion.9
  277.9 11.7 %cholesky.16 = f32[128,128]{1,0:T(8,128)S(1)} custom-call(f32[128,128]{1,0:T(8,128)S(1)} %fusion.9), custom_call_target="Cholesky" | custom-call | tf_op jit(solution)/shard_map/jit(cholesky)/cholesky | solution.py:32
  289.7 0.6 compare_reduce_fusion
  290.3 0.7 fusion.7
  291.0 9.8 %custom-call.6 = f32[1,128,128]{1,2,0:T(8,128)S(1)} custom-call(f32[1,128,128]{2,1,0:T(8,128)S(1)} %fusion.7), custom_call_target="InvertDiagBlocksLowerTriangular" | custom-call | tf_op jit(solution)/shard_map/triangular_solve | solution.py:33
  300.8 2.1 fusion.3
  (6 shorter events, 0.1 us)
Async XLA Ops:
  6.5 3.9 %copy-start.1 = (s32[32,1]{0,1:T(1,128)S(1)}, s32[32,1]{0,1:T(1,128)}, u32[]{:S(2)}) copy-start(s32[32,1]{0,1:T(1,128)} %param.5) | copy-start | bytes 388
  6.5 99.6 %all-reduce.3.cloned.1.call-start = ((), (), s32[]{:S(2)}) async-start(), calls=%async_computation.1 | async-start | bytes 2097152 | tf_op jit(solution)/shard_map/psum | solution.py:19
  10.3 125.7 %reduce-scatter.2.cloned.1.call-start = ((), (), s32[]{:S(2)}) async-start(), calls=%async_computation.2 | async-start | bytes 983040 | tf_op jit(solution)/shard_map/reduce_scatter | solution.py:29
  109.0 9.4 %copy-start = (f32[2048,128]{1,0:T(8,128)S(1)}, f32[2048,128]{1,0:T(8,128)}, u32[]{:S(2)}) copy-start(f32[2048,128]{1,0:T(8,128)} %all-reduce.3.cloned.1.call-done) | copy-start | bytes 3145732
  121.2 154.9 %all-reduce.5.cloned.1.call-start = ((), (), s32[]{:S(2)}) async-start(), calls=%async_computation.3 | async-start | bytes 655360 | tf_op jit(solution)/shard_map/psum | solution.py:30
Sparse Core Ops, SparseCore 0:
  10.4 95.6 all-reduce.2
  121.3 14.6 reduce-scatter.1
  138.6 137.4 all-reduce.4
where the time goes:
time: 310 us; the launch traced here: 309 us
  waiting for transfers between devices  239 us (77%)
  other arithmetic  31 us (10%)
  matrix products  13.4 us (4%)
  between operations  13.2 us (4%)
  local copies, waits for them, and re-layouts  13 us (4%)
    psum x1, waiting for transfers between devices, per_device(): sums = lax.psum(sums, 'row')  140 us
    psum x1, waiting for transfers between devices, per_device(): panel = lax.psum(panel, 'col')  84 us
    reduce_scatter x1, waiting for transfers between devices, per_device(): sums = lax.psum_scatter(sums, 'leaf', scatter_dimension=0, tiled=True)  14.5 us
    another operation x3, other arithmetic, per_device(): lower = jnp.linalg.cholesky(gram)  12.4 us
    mul x2, local copies, waits for them, and re-layouts, per_device(): tiles.reshape(tile_count, edge, blocks_dev, edge) * mask[:, None, :, None]  11.3 us
    dot_general x2, matrix products, per_device(): lax.dot_general(a, b, (((0,), (0,)), ((), ())), precision=lax.Precision.H...  11.3 us
    another operation x2, other arithmetic, per_device(): top = lax.linalg.triangular_solve(lower, cross, left_side=True, lower=True)  10.5 us
  transfers between devices with their start and end apart: 3, of which 3 were waited for; matrix products, arithmetic and copies ran while one was open for 4% of the time, Pallas kernels for 0%

commit v1 on v0

--- a/solution.py
+++ b/solution.py
@@ -27,7 +27,7 @@
     )
     sums = jnp.concatenate([dot(left, masked), dot(left, panel)], axis=1)
     sums = lax.psum_scatter(sums, "leaf", scatter_dimension=0, tiled=True)
-    sums = lax.psum(sums, "row")
+    sums = jnp.sum(lax.all_gather(sums, "row"), axis=0)
     cross, gram = (sums[:, :columns_dev], sums[:, columns_dev:])
     lower = jnp.linalg.cholesky(gram)
     top = lax.linalg.triangular_solve(lower, cross, left_side=True, lower=True)

time: 310 us -> 296 us (0.955)
  waiting for transfers between devices: 239 us -> 221 us
    psum x1 -> x0, waiting for transfers between devices: 140 us -> none  [per_device(): sums = lax.psum(sums, 'row')]
    all_gather x0 -> x1, waiting for transfers between devices: none -> 122 us  [per_device(): sums = jnp.sum(lax.all_gather(sums, 'row'), axis=0)]
where the time goes in v1:
time: 296 us; the launch traced here: 293 us
  waiting for transfers between devices  221 us (75%)
  other arithmetic  32.9 us (11%)
  matrix products  13.9 us (5%)
  between operations  13.2 us (4%)
  local copies, waits for them, and re-layouts  12.1 us (4%)
    all_gather x1, waiting for transfers between devices, per_device(): sums = jnp.sum(lax.all_gather(sums, 'row'), axis=0)  122 us
    psum x1, waiting for transfers between devices, per_device(): panel = lax.psum(panel, 'col')  84 us
    reduce_scatter x1, waiting for transfers between devices, per_device(): sums = lax.psum_scatter(sums, 'leaf', scatter_dimension=0, tiled=True)  14.5 us
    dot_general x2, matrix products, per_device(): lax.dot_general(a, b, (((0,), (0,)), ((), ())), precision=lax.Precision.H...  12.8 us
    another operation x3, other arithmetic, per_device(): lower = jnp.linalg.cholesky(gram)  12.4 us
    mul x2, local copies, waits for them, and re-layouts, per_device(): tiles.reshape(tile_count, edge, blocks_dev, edge) * mask[:, None, :, None]  11.3 us
    another operation x2, other arithmetic, per_device(): top = lax.linalg.triangular_solve(lower, cross, left_side=True, lower=True)  10.5 us
  transfers between devices with their start and end apart: 3, of which 3 were waited for; matrix products, arithmetic and copies ran while one was open for 4% of the time, Pallas kernels for 0%

profile of v1, /device:TPU:6, one launch (start us, length us, event | category | flops | bytes accessed | tf_op | source)
XLA Modules:
  0.0 293.4 jit_solution(4315545489613592043)
XLA Ops:
  6.5 0.0 copy-start.1
  6.5 0.0 all-reduce.2.cloned.1.call-start
  6.5 0.7 convert_element_type.3
  7.2 0.1 broadcast_in_dim.48
  7.3 0.1 mul.25
  7.4 1.6 fusion.5
  9.0 1.3 pad_maximum_fusion.3
  10.3 0.0 all-reduce.2.cloned.1.call-update
  10.3 0.0 reduce-scatter.2.cloned.1.call-start
  10.3 0.1 copy.7
  10.4 0.0 copy-done.1
  10.5 0.1 broadcast_in_dim.51
  10.5 0.1 eq.37
  10.6 0.1 broadcast_in_dim.46
  10.7 0.1 eq.33
  10.8 3.8 %mul.28 = f32[32,64,8,64]{3,2,1,0:T(8,128)} broadcast(f32[32,8]{1,0:T(8,128)S(1)} %copy.7), dimensions={0,2} | broadcast | bytes 4195328 | tf_op jit(solution)/shard_map/mul | solution.py:22
  14.6 7.5 %mul.29 = f32[2048,512]{1,0:T(8,128)} reshape(f32[32,64,8,64]{3,2,1,0:T(8,128)} %mul.28) | data formatting | bytes 8388608 | tf_op jit(solution)/shard_map/mul | solution.py:22
  22.1 84.0 %all-reduce.2.cloned.1.call-done = f32[2048,128]{1,0:T(8,128)} async-done(((f32[2048,128]{1,0:T(8,128)}), f32[2048,128]{1,0:T(8,128)}) %all-reduce.2.cloned.1.call-update) | async-done | bytes 1048592 | tf_op jit(solution)/shard_map/psum | solution.py:19
  106.1 2.8 broadcast_select_fusion.1
  109.0 0.0 copy-start
  109.0 9.4 %fusion = f32[256,512]{1,0:T(8,128)S(1)} fusion(f32[2048,512]{1,0:T(8,128)} %bitcast.28, f32[2048,512]{1,0:T(8,128)} %mul.29, f32[2048,128]{1,0:T(8,128)S(1)} %get-tuple-element.10, f32[2048,128]{1,0:T(8,128)S(1)} %get-tuple-element.9), kind=kOutput, calls=%fused_computation | convolution fusion | flops 3222798336 | bytes 11010048 | tf_op jit(solution)/shard_map/dot_general | solution.py:25
  118.4 0.0 copy-done
  118.4 3.4 %fusion.2 = f32[256,128]{1,0:T(8,128)S(1)} fusion(f32[2048,128]{1,0:T(8,128)S(1)} %copy-done, f32[2048,128]{1,0:T(8,128)S(1)} %get-tuple-element.10, f32[2048,128]{1,0:T(8,128)S(1)} %get-tuple-element.9), kind=kOutput, calls=%fused_computation.3 | convolution fusion | flops 805830656 | bytes 3276800 | tf_op jit(solution)/shard_map/dot_general | solution.py:25
  121.8 0.9 pad_maximum_fusion.4
  122.7 0.0 reduce-scatter.2.cloned.1.call-update
  122.7 0.2 all-gather.3.cloned.1.call-start
  122.9 14.5 %reduce-scatter.2.cloned.1.call-done = f32[128,640]{1,0:T(8,128)} async-done(((f32[256,640]{1,0:T(8,128)}), f32[128,640]{1,0:T(8,128)}) %reduce-scatter.2.cloned.1.call-update) | async-done | bytes 327696 | tf_op jit(solution)/shard_map/reduce_scatter | solution.py:29
  137.5 0.0 all-gather.3.cloned.1.call-update
  137.5 0.1 broadcast_in_dim.45
  137.6 0.1 ge.17
  137.7 122.3 %all-gather.3.cloned.1.call-done = f32[2048,640]{1,0:T(8,128)} async-done(((f32[128,640]{1,0:T(8,128)}), f32[2048,640]{1,0:T(8,128)}) %all-gather.3.cloned.1.call-update) | async-done | bytes 5242896 | tf_op jit(solution)/shard_map/all_gather | solution.py:30
  260.0 2.8 reduce_sum.9
  262.8 0.1 copy.12
  262.9 11.7 %cholesky.16 = f32[128,128]{1,0:T(8,128)S(1)} custom-call(f32[128,128]{1,0:T(8,128)S(1)} %fusion.9), custom_call_target="Cholesky" | custom-call | tf_op jit(solution)/shard_map/jit(cholesky)/cholesky | solution.py:32
  274.7 0.6 compare_reduce_fusion
  275.3 0.7 fusion.7
  276.0 9.8 %custom-call.6 = f32[1,128,128]{1,2,0:T(8,128)S(1)} custom-call(f32[1,128,128]{2,1,0:T(8,128)S(1)} %fusion.7), custom_call_target="InvertDiagBlocksLowerTriangular" | custom-call | tf_op jit(solution)/shard_map/triangular_solve | solution.py:33
  285.8 1.1 fusion.3
  (8 shorter events, 0.1 us)
Async XLA Ops:
  6.5 3.9 %copy-start.1 = (s32[32,1]{0,1:T(1,128)S(1)}, s32[32,1]{0,1:T(1,128)}, u32[]{:S(2)}) copy-start(s32[32,1]{0,1:T(1,128)} %param.5) | copy-start | bytes 388
  6.5 99.6 %all-reduce.2.cloned.1.call-start = ((), (), s32[]{:S(2)}) async-start(), calls=%async_computation.1 | async-start | bytes 2097152 | tf_op jit(solution)/shard_map/psum | solution.py:19
  10.3 127.2 %reduce-scatter.2.cloned.1.call-start = ((), (), s32[]{:S(2)}) async-start(), calls=%async_computation.2 | async-start | bytes 983040 | tf_op jit(solution)/shard_map/reduce_scatter | solution.py:29
  109.0 9.4 %copy-start = (f32[2048,128]{1,0:T(8,128)S(1)}, f32[2048,128]{1,0:T(8,128)}, u32[]{:S(2)}) copy-start(f32[2048,128]{1,0:T(8,128)} %all-reduce.2.cloned.1.call-done) | copy-start | bytes 3145732
  122.7 137.3 %all-gather.3.cloned.1.call-start = ((), (), s32[]{:S(2)}) async-start(), calls=%async_computation.3 | async-start | bytes 5570560 | tf_op jit(solution)/shard_map/all_gather | solution.py:30
Sparse Core Ops, SparseCore 0:
  10.4 95.6 all-reduce.1
  122.8 14.6 reduce-scatter.1
  139.3 120.6 all-gather.2
